TPU v7x, 32 devices: a whole 2x2x4 slice. The times are simulated.
32 devices in a mesh: pair: 2 (over x), grow: 4 (over y, core), gcol: 4 (over z).
Axes of the slice: x: 2, y: 2, z: 4, core: 2. Of those that a mesh axis runs over, the one named last changes fastest.
Arguments:
- core_matrix: bfloat16 [12288, 12288], P('grow', 'gcol'), may hold values from -0.00048828125 to 0.00048828125
- pair_panels: bfloat16 [12, 32, 12288], P('pair', None, ('grow', 'gcol')), may hold values from -6 to 6
- amplitudes: bfloat16 [12, 32, 32], P('pair'), may hold values from -0.1875 to 0.1875
- pair_widths: int32 [12], P('pair'), may hold values from 8 to 32
- batch_plan: int32 [12], P('pair'), may hold values from 0 to 11, each once
Outputs:
- residual: float32 [12, 1024], P('pair', ('grow', 'gcol'))
Inputs may be any that keep to these rules, and one draw needn't show every extreme that they name: batch_plan names every pair exactly once.
All inputs are finite; a program needn't handle non-finite values.
Results may differ from a plain program's by a relative error of at most 0.015.
Values may be sent and summed in bfloat16 or wider, within the bound.
A program may use at most 64 MiB of HBM per device.

v0:
```python
import jax
import jax.numpy as jnp
from jax import lax
from jax.sharding import PartitionSpec as P


def local(core_matrix, pair_panels, amplitudes, pair_widths, batch_plan):
    depth = amplitudes.shape[1]
    live = (
        lax.broadcasted_iota(jnp.int32, (pair_widths.shape[0], depth), 1) < pair_widths[:, None]
    ).astype(jnp.bfloat16)
    masked = amplitudes * live[:, :, None] * live[:, None, :]
    row_index = lax.axis_index("grow")
    col_index = lax.axis_index("gcol")
    row_len = core_matrix.shape[0]
    col_len = core_matrix.shape[1]
    gathered = lax.all_gather(pair_panels, ("grow", "gcol"), axis=2, tiled=True)
    left = lax.dynamic_slice_in_dim(gathered, row_index * row_len, row_len, 2)
    right = lax.dynamic_slice_in_dim(gathered, col_index * col_len, col_len, 2)

    def slot_term(items):
        left_panel, right_panel, amps, mask = items
        projected = jnp.dot(amps, right_panel, preferred_element_type=jnp.float32).astype(
            jnp.bfloat16
        )
        coupled = lax.dot_general(
            left_panel, projected, (((0,), (0,)), ((), ())), preferred_element_type=jnp.float32
        ).astype(jnp.bfloat16)
        coupled = lax.optimization_barrier(coupled)
        weighted = (core_matrix.astype(jnp.float32) * coupled.astype(jnp.float32)).astype(
            jnp.bfloat16
        )
        back = lax.dot_general(
            weighted, right_panel, (((1,), (1,)), ((), ())), preferred_element_type=jnp.float32
        ).astype(jnp.bfloat16)
        partial_sum = jnp.dot(left_panel, back, preferred_element_type=jnp.float32)
        keep = mask.astype(jnp.float32)
        return (partial_sum * keep[:, None] * keep[None, :]).reshape(depth * depth)

    terms = lax.map(slot_term, (left, right, masked, live))
    total = lax.psum(terms, ("grow", "gcol"))
    share = terms.shape[1] // lax.axis_size(("grow", "gcol"))
    reduced = lax.dynamic_slice_in_dim(total, lax.axis_index(("grow", "gcol")) * share, share, 1)
    every_row = lax.all_gather(reduced, "pair", axis=0, tiled=True)
    return jnp.take(every_row, batch_plan, axis=0)


def solution(mesh):
    in_specs = (
        P("grow", "gcol"),
        P("pair", None, ("grow", "gcol")),
        P("pair", None, None),
        P("pair"),
        P("pair"),
    )
    out_specs = P("pair", ("grow", "gcol"))
    return jax.shard_map(local, mesh=mesh, in_specs=in_specs, out_specs=out_specs, check_vma=False)
```

profile of v0, /device:TPU:0, one launch (start us, length us, event | category | flops | bytes accessed | tf_op | source)
XLA Modules:
  0.0 285.3 jit_solution(8804718714653839679)
XLA Ops:
  6.5 0.0 all-gather.3.cloned.1.call-start
  6.5 0.7 all-gather.3.cloned.1.call-update
  7.3 0.7 compare_select_fusion
  8.0 0.7 compare_and_fusion
  8.6 0.7 fusion.27
  9.3 0.9 multiply_multiply_fusion
  10.2 55.5 %all-gather.3.cloned.1.call-done = bf16[6,32,12288]{2,1,0:T(8,128)(2,1)} async-done(((bf16[6,32,768]{2,1,0:T(8,128)(2,1)}), bf16[6,32,12288]{2,1,0:T(8,128)(2,1)}) %all-gather.3.cloned.1.call-update) | async-done | bytes 4718608 | tf_op jit(solution)/shard_map/all_gather | solution.py:17
  65.8 1.9 constant_dynamic-slice_fusion.1
  67.6 145.8 %while.10 = (s32[]{:T(128)}, f32[6,1024]{1,0:T(8,128)S(1)}, bf16[6,32,3072]{2,1,0:T(8,128)(2,1)S(1)}, bf16[3072,3072]{1,0:T(8,128)(2,1)}, bf16[6,32,32]{2,1,0:T(...) while((s32[]{:T(128)}, f32[6,1024]{1,0:T(8,128)S(1)}, ...), condition=%wide.region_1.2_spmd, body=%wide.region_0.1_spmd.sunk | while | flops 1267927040 | bytes 57442084 | solution.py:40
  67.6 9.3 %convolution_convert_fusion.3 = bf16[3072,3072]{1,0:T(8,128)(2,1)} fusion(bf16[6,32,3072]{2,1,0:T(8,128)(2,1)S(1)} %get-tuple-element.125, s32[]{:T(128)} %get-tuple-element.111, bf16[6,32,3072]{2,1,0:T(8,128)(2,1)S(1)} %get-tuple-element.122, bf16[6,32,32]{2,1,0:T(8,128)(2,1)S(1)} %get-tuple-element.124), kind=kOutput, calls=%fused_computation.3.clone.1 | convolution fusion | flops 619806720 | bytes 19277312 | tf_op jit(solution)/shard_map/while/body/eval_jaxpr/dot_general | solution.py:26
  77.0 14.8 %fusion.41 = f32[32,32]{1,0:T(8,128)S(1)} fusion(bf16[3072,3072]{1,0:T(8,128)(2,1)} %convolution_convert_fusion.3, bf16[3072,3072]{1,0:T(8,128)(2,1)} %get-tuple-element.123, bf16[6,32,3072]{2,1,0:T(8,128)(2,1)S(1)} %get-tuple-element.125, s32[]{:T(128)} %get-tuple-element.111, bf16[6,32,3072]{2,1,0:T(8,128)(2,1)S(1)} %get-tuple-element.122, ...), kind=kOutput, calls=%fused_computation.8.clone.1 | convolution fusion | flops 648120320 | bytes 38148096 | tf_op jit(solution)/shard_map/while/body/eval_jaxpr/dot_general | solution.py:36
  91.8 0.1 broadcast_in_dim.31
  91.8 0.1 dynamic_update_slice.5
  91.9 9.3 %convolution_convert_fusion.3 = bf16[3072,3072]{1,0:T(8,128)(2,1)} fusion(bf16[6,32,3072]{2,1,0:T(8,128)(2,1)S(1)} %get-tuple-element.125, s32[]{:T(128)} %get-tuple-element.111, bf16[6,32,3072]{2,1,0:T(8,128)(2,1)S(1)} %get-tuple-element.122, bf16[6,32,32]{2,1,0:T(8,128)(2,1)S(1)} %get-tuple-element.124), kind=kOutput, calls=%fused_computation.3.clone.1 | convolution fusion | flops 619806720 | bytes 19277312 | tf_op jit(solution)/shard_map/while/body/eval_jaxpr/dot_general | solution.py:26
  101.3 14.8 %fusion.41 = f32[32,32]{1,0:T(8,128)S(1)} fusion(bf16[3072,3072]{1,0:T(8,128)(2,1)} %convolution_convert_fusion.3, bf16[3072,3072]{1,0:T(8,128)(2,1)} %get-tuple-element.123, bf16[6,32,3072]{2,1,0:T(8,128)(2,1)S(1)} %get-tuple-element.125, s32[]{:T(128)} %get-tuple-element.111, bf16[6,32,3072]{2,1,0:T(8,128)(2,1)S(1)} %get-tuple-element.122, ...), kind=kOutput, calls=%fused_computation.8.clone.1 | convolution fusion | flops 648120320 | bytes 38148096 | tf_op jit(solution)/shard_map/while/body/eval_jaxpr/dot_general | solution.py:36
  116.1 0.1 broadcast_in_dim.31
  116.1 0.1 dynamic_update_slice.5
  116.2 9.3 %convolution_convert_fusion.3 = bf16[3072,3072]{1,0:T(8,128)(2,1)} fusion(bf16[6,32,3072]{2,1,0:T(8,128)(2,1)S(1)} %get-tuple-element.125, s32[]{:T(128)} %get-tuple-element.111, bf16[6,32,3072]{2,1,0:T(8,128)(2,1)S(1)} %get-tuple-element.122, bf16[6,32,32]{2,1,0:T(8,128)(2,1)S(1)} %get-tuple-element.124), kind=kOutput, calls=%fused_computation.3.clone.1 | convolution fusion | flops 619806720 | bytes 19277312 | tf_op jit(solution)/shard_map/while/body/eval_jaxpr/dot_general | solution.py:26
  125.6 14.8 %fusion.41 = f32[32,32]{1,0:T(8,128)S(1)} fusion(bf16[3072,3072]{1,0:T(8,128)(2,1)} %convolution_convert_fusion.3, bf16[3072,3072]{1,0:T(8,128)(2,1)} %get-tuple-element.123, bf16[6,32,3072]{2,1,0:T(8,128)(2,1)S(1)} %get-tuple-element.125, s32[]{:T(128)} %get-tuple-element.111, bf16[6,32,3072]{2,1,0:T(8,128)(2,1)S(1)} %get-tuple-element.122, ...), kind=kOutput, calls=%fused_computation.8.clone.1 | convolution fusion | flops 648120320 | bytes 38148096 | tf_op jit(solution)/shard_map/while/body/eval_jaxpr/dot_general | solution.py:36
  140.3 0.1 broadcast_in_dim.31
  140.4 0.1 dynamic_update_slice.5
  140.5 9.3 %convolution_convert_fusion.3 = bf16[3072,3072]{1,0:T(8,128)(2,1)} fusion(bf16[6,32,3072]{2,1,0:T(8,128)(2,1)S(1)} %get-tuple-element.125, s32[]{:T(128)} %get-tuple-element.111, bf16[6,32,3072]{2,1,0:T(8,128)(2,1)S(1)} %get-tuple-element.122, bf16[6,32,32]{2,1,0:T(8,128)(2,1)S(1)} %get-tuple-element.124), kind=kOutput, calls=%fused_computation.3.clone.1 | convolution fusion | flops 619806720 | bytes 19277312 | tf_op jit(solution)/shard_map/while/body/eval_jaxpr/dot_general | solution.py:26
  149.9 14.8 %fusion.41 = f32[32,32]{1,0:T(8,128)S(1)} fusion(bf16[3072,3072]{1,0:T(8,128)(2,1)} %convolution_convert_fusion.3, bf16[3072,3072]{1,0:T(8,128)(2,1)} %get-tuple-element.123, bf16[6,32,3072]{2,1,0:T(8,128)(2,1)S(1)} %get-tuple-element.125, s32[]{:T(128)} %get-tuple-element.111, bf16[6,32,3072]{2,1,0:T(8,128)(2,1)S(1)} %get-tuple-element.122, ...), kind=kOutput, calls=%fused_computation.8.clone.1 | convolution fusion | flops 648120320 | bytes 38148096 | tf_op jit(solution)/shard_map/while/body/eval_jaxpr/dot_general | solution.py:36
  164.6 0.1 broadcast_in_dim.31
  164.7 0.1 dynamic_update_slice.5
  164.8 9.3 %convolution_convert_fusion.3 = bf16[3072,3072]{1,0:T(8,128)(2,1)} fusion(bf16[6,32,3072]{2,1,0:T(8,128)(2,1)S(1)} %get-tuple-element.125, s32[]{:T(128)} %get-tuple-element.111, bf16[6,32,3072]{2,1,0:T(8,128)(2,1)S(1)} %get-tuple-element.122, bf16[6,32,32]{2,1,0:T(8,128)(2,1)S(1)} %get-tuple-element.124), kind=kOutput, calls=%fused_computation.3.clone.1 | convolution fusion | flops 619806720 | bytes 19277312 | tf_op jit(solution)/shard_map/while/body/eval_jaxpr/dot_general | solution.py:26
  174.2 14.8 %fusion.41 = f32[32,32]{1,0:T(8,128)S(1)} fusion(bf16[3072,3072]{1,0:T(8,128)(2,1)} %convolution_convert_fusion.3, bf16[3072,3072]{1,0:T(8,128)(2,1)} %get-tuple-element.123, bf16[6,32,3072]{2,1,0:T(8,128)(2,1)S(1)} %get-tuple-element.125, s32[]{:T(128)} %get-tuple-element.111, bf16[6,32,3072]{2,1,0:T(8,128)(2,1)S(1)} %get-tuple-element.122, ...), kind=kOutput, calls=%fused_computation.8.clone.1 | convolution fusion | flops 648120320 | bytes 38148096 | tf_op jit(solution)/shard_map/while/body/eval_jaxpr/dot_general | solution.py:36
  188.9 0.1 broadcast_in_dim.31
  189.0 0.1 dynamic_update_slice.5
  189.1 9.3 %convolution_convert_fusion.3 = bf16[3072,3072]{1,0:T(8,128)(2,1)} fusion(bf16[6,32,3072]{2,1,0:T(8,128)(2,1)S(1)} %get-tuple-element.125, s32[]{:T(128)} %get-tuple-element.111, bf16[6,32,3072]{2,1,0:T(8,128)(2,1)S(1)} %get-tuple-element.122, bf16[6,32,32]{2,1,0:T(8,128)(2,1)S(1)} %get-tuple-element.124), kind=kOutput, calls=%fused_computation.3.clone.1 | convolution fusion | flops 619806720 | bytes 19277312 | tf_op jit(solution)/shard_map/while/body/eval_jaxpr/dot_general | solution.py:26
  198.5 14.8 %fusion.41 = f32[32,32]{1,0:T(8,128)S(1)} fusion(bf16[3072,3072]{1,0:T(8,128)(2,1)} %convolution_convert_fusion.3, bf16[3072,3072]{1,0:T(8,128)(2,1)} %get-tuple-element.123, bf16[6,32,3072]{2,1,0:T(8,128)(2,1)S(1)} %get-tuple-element.125, s32[]{:T(128)} %get-tuple-element.111, bf16[6,32,3072]{2,1,0:T(8,128)(2,1)S(1)} %get-tuple-element.122, ...), kind=kOutput, calls=%fused_computation.8.clone.1 | convolution fusion | flops 648120320 | bytes 38148096 | tf_op jit(solution)/shard_map/while/body/eval_jaxpr/dot_general | solution.py:36
  213.2 0.1 broadcast_in_dim.31
  213.3 0.1 dynamic_update_slice.5
  213.4 59.4 %psum.7 = f32[6,1024]{1,0:T(8,128)S(1)} all-reduce(f32[6,1024]{1,0:T(8,128)S(1)} %get-tuple-element.42), channel_id=1, replica_groups=mesh['pair'=2,'grow'=4,'gcol'=4] {'grow','gcol'}, use_global_device_ids=true, to_apply=%region_2.3 | all-reduce | flops 6144 | bytes 49152 | tf_op jit(solution)/shard_map/psum | solution.py:41
  272.8 0.1 dynamic-slice_bitcast_fusion
  272.9 4.3 %all-gather = f32[2,6,64]{2,1,0:T(8,128)S(1)} all-gather(f32[1,6,64]{2,1,0:T(8,128)S(1)} %dynamic-slice_bitcast_fusion), channel_id=1, replica_groups=mesh['pair'=2,'grow'=4,'gcol'=4] {'pair'}, dimensions={0}, use_global_device_ids=true | all-gather | bytes 4608 | tf_op jit(solution)/shard_map/all_gather | solution.py:44
  277.2 0.6 gather_fusion
  277.8 0.7 broadcast_select_fusion
  (9 shorter events, 0.0 us)
Async XLA Ops:
  6.5 59.2 %all-gather.3.cloned.1.call-start = ((), (), s32[]{:S(2)}) async-start(), calls=%async_computation | async-start | bytes 5013504 | tf_op jit(solution)/shard_map/all_gather | solution.py:17
Sparse Core Ops, SparseCore 0:
  9.5 56.1 all-gather.2
where the time goes:
time: 286 us; the launch traced here: 285 us
  matrix products  145 us (51%)
  blocking collectives  63.7 us (22%)
  waiting for transfers between devices  56.2 us (20%)
  between operations  13.4 us (5%)
  other arithmetic  3.64 us (1%)
  local copies, waits for them, and re-layouts  3.44 us (1%)
    dot_general x6, matrix products, slot_term(): partial_sum = jnp.dot(left_panel, back, preferred_element_type=jnp.float32)  88.5 us
    psum x1, blocking collectives, local(): total = lax.psum(terms, ('grow', 'gcol'))  59.4 us
    dot_general x6, matrix products, slot_term(): lax.dot_general(left_panel, projected, (((0,), (0,)), ((), ())), preferre...  56.1 us
    all_gather x1, waiting for transfers between devices, local(): gathered = lax.all_gather(pair_panels, ('grow', 'gcol'), axis=2, tiled=True)  55.5 us
  transfers between devices with their start and end apart: 1, of which 1 were waited for; matrix products, arithmetic and copies ran while one was open for 1% of the time, Pallas kernels for 0%

commit v1 on v0

--- a/solution.py
+++ b/solution.py
@@ -2,6 +2,11 @@
 import jax.numpy as jnp
 from jax import lax
 from jax.sharding import PartitionSpec as P
+
+
+def _meet_surface(z_in):
+    high = lax.psum(lax.psum(z_in, "grow"), "gcol")
+    return high
 
 
 def local(core_matrix, pair_panels, amplitudes, pair_widths, batch_plan):
@@ -38,7 +43,7 @@
         return (partial_sum * keep[:, None] * keep[None, :]).reshape(depth * depth)
 
     terms = lax.map(slot_term, (left, right, masked, live))
-    total = lax.psum(terms, ("grow", "gcol"))
+    total = _meet_surface(terms)
     share = terms.shape[1] // lax.axis_size(("grow", "gcol"))
     reduced = lax.dynamic_slice_in_dim(total, lax.axis_index(("grow", "gcol")) * share, share, 1)
     every_row = lax.all_gather(reduced, "pair", axis=0, tiled=True)

time: 286 us -> 254 us (0.89)
  blocking collectives: 63.7 us -> 32.2 us
    psum x1 -> x2, blocking collectives: 59.4 us -> 27.8 us  [_meet_surface(): high = lax.psum(lax.psum(z_in, 'grow'), 'gcol')]
where the time goes in v1:
time: 254 us
  matrix products  145 us (57%)
  waiting for transfers between devices  56.2 us (22%)
  blocking collectives  32.2 us (13%)
  between operations  13.5 us (5%)
  other arithmetic  3.64 us (1%)
  local copies, waits for them, and re-layouts  3.51 us (1%)
    dot_general x6, matrix products, slot_term(): partial_sum = jnp.dot(left_panel, back, preferred_element_type=jnp.float32)  88.5 us
    dot_general x6, matrix products, slot_term(): lax.dot_general(left_panel, projected, (((0,), (0,)), ((), ())), preferre...  56.1 us
    all_gather x1, waiting for transfers between devices, local(): gathered = lax.all_gather(pair_panels, ('grow', 'gcol'), axis=2, tiled=True)  55.5 us
    psum x2, blocking collectives, _meet_surface(): high = lax.psum(lax.psum(z_in, 'grow'), 'gcol')  27.8 us
  transfers between devices with their start and end apart: 1, of which 1 were waited for; matrix products, arithmetic and copies ran while one was open for 1% of the time, Pallas kernels for 0%

profile of v1, /device:TPU:0, one launch (start us, length us, event | category | flops | bytes accessed | tf_op | source)
XLA Modules:
  0.0 253.8 jit_solution(17306189522465135303)
XLA Ops:
  6.5 0.0 all-gather.3.cloned.1.call-start
  6.5 0.7 all-gather.3.cloned.1.call-update
  7.3 0.7 compare_select_fusion
  8.0 0.7 compare_and_fusion
  8.6 0.7 fusion.27
  9.3 0.9 multiply_multiply_fusion
  10.2 55.5 %all-gather.3.cloned.1.call-done = bf16[6,32,12288]{2,1,0:T(8,128)(2,1)} async-done(((bf16[6,32,768]{2,1,0:T(8,128)(2,1)}), bf16[6,32,12288]{2,1,0:T(8,128)(2,1)}) %all-gather.3.cloned.1.call-update) | async-done | bytes 4718608 | tf_op jit(solution)/shard_map/all_gather | solution.py:22
  65.8 1.9 constant_dynamic-slice_fusion.1
  67.7 145.8 %while.10 = (s32[]{:T(128)}, f32[6,1024]{1,0:T(8,128)S(1)}, bf16[6,32,3072]{2,1,0:T(8,128)(2,1)S(1)}, bf16[3072,3072]{1,0:T(8,128)(2,1)}, bf16[6,32,32]{2,1,0:T(...) while((s32[]{:T(128)}, f32[6,1024]{1,0:T(8,128)S(1)}, ...), condition=%wide.region_1.2_spmd, body=%wide.region_0.1_spmd.sunk | while | flops 1267927040 | bytes 57442084 | solution.py:45
  67.7 9.4 %convolution_convert_fusion.3 = bf16[3072,3072]{1,0:T(8,128)(2,1)} fusion(bf16[6,32,3072]{2,1,0:T(8,128)(2,1)S(1)} %get-tuple-element.125, s32[]{:T(128)} %get-tuple-element.111, bf16[6,32,3072]{2,1,0:T(8,128)(2,1)S(1)} %get-tuple-element.122, bf16[6,32,32]{2,1,0:T(8,128)(2,1)S(1)} %get-tuple-element.124), kind=kOutput, calls=%fused_computation.3.clone.1 | convolution fusion | flops 619806720 | bytes 19277312 | tf_op jit(solution)/shard_map/while/body/eval_jaxpr/dot_general | solution.py:31
  77.1 14.8 %fusion.41 = f32[32,32]{1,0:T(8,128)S(1)} fusion(bf16[3072,3072]{1,0:T(8,128)(2,1)} %convolution_convert_fusion.3, bf16[3072,3072]{1,0:T(8,128)(2,1)} %get-tuple-element.123, bf16[6,32,3072]{2,1,0:T(8,128)(2,1)S(1)} %get-tuple-element.125, s32[]{:T(128)} %get-tuple-element.111, bf16[6,32,3072]{2,1,0:T(8,128)(2,1)S(1)} %get-tuple-element.122, ...), kind=kOutput, calls=%fused_computation.8.clone.1 | convolution fusion | flops 648120320 | bytes 38148096 | tf_op jit(solution)/shard_map/while/body/eval_jaxpr/dot_general | solution.py:41
  91.8 0.1 broadcast_in_dim.31
  91.9 0.1 dynamic_update_slice.5
  92.0 9.4 %convolution_convert_fusion.3 = bf16[3072,3072]{1,0:T(8,128)(2,1)} fusion(bf16[6,32,3072]{2,1,0:T(8,128)(2,1)S(1)} %get-tuple-element.125, s32[]{:T(128)} %get-tuple-element.111, bf16[6,32,3072]{2,1,0:T(8,128)(2,1)S(1)} %get-tuple-element.122, bf16[6,32,32]{2,1,0:T(8,128)(2,1)S(1)} %get-tuple-element.124), kind=kOutput, calls=%fused_computation.3.clone.1 | convolution fusion | flops 619806720 | bytes 19277312 | tf_op jit(solution)/shard_map/while/body/eval_jaxpr/dot_general | solution.py:31
  101.4 14.8 %fusion.41 = f32[32,32]{1,0:T(8,128)S(1)} fusion(bf16[3072,3072]{1,0:T(8,128)(2,1)} %convolution_convert_fusion.3, bf16[3072,3072]{1,0:T(8,128)(2,1)} %get-tuple-element.123, bf16[6,32,3072]{2,1,0:T(8,128)(2,1)S(1)} %get-tuple-element.125, s32[]{:T(128)} %get-tuple-element.111, bf16[6,32,3072]{2,1,0:T(8,128)(2,1)S(1)} %get-tuple-element.122, ...), kind=kOutput, calls=%fused_computation.8.clone.1 | convolution fusion | flops 648120320 | bytes 38148096 | tf_op jit(solution)/shard_map/while/body/eval_jaxpr/dot_general | solution.py:41
  116.1 0.1 broadcast_in_dim.31
  116.2 0.1 dynamic_update_slice.5
  116.3 9.4 %convolution_convert_fusion.3 = bf16[3072,3072]{1,0:T(8,128)(2,1)} fusion(bf16[6,32,3072]{2,1,0:T(8,128)(2,1)S(1)} %get-tuple-element.125, s32[]{:T(128)} %get-tuple-element.111, bf16[6,32,3072]{2,1,0:T(8,128)(2,1)S(1)} %get-tuple-element.122, bf16[6,32,32]{2,1,0:T(8,128)(2,1)S(1)} %get-tuple-element.124), kind=kOutput, calls=%fused_computation.3.clone.1 | convolution fusion | flops 619806720 | bytes 19277312 | tf_op jit(solution)/shard_map/while/body/eval_jaxpr/dot_general | solution.py:31
  125.7 14.8 %fusion.41 = f32[32,32]{1,0:T(8,128)S(1)} fusion(bf16[3072,3072]{1,0:T(8,128)(2,1)} %convolution_convert_fusion.3, bf16[3072,3072]{1,0:T(8,128)(2,1)} %get-tuple-element.123, bf16[6,32,3072]{2,1,0:T(8,128)(2,1)S(1)} %get-tuple-element.125, s32[]{:T(128)} %get-tuple-element.111, bf16[6,32,3072]{2,1,0:T(8,128)(2,1)S(1)} %get-tuple-element.122, ...), kind=kOutput, calls=%fused_computation.8.clone.1 | convolution fusion | flops 648120320 | bytes 38148096 | tf_op jit(solution)/shard_map/while/body/eval_jaxpr/dot_general | solution.py:41
  140.4 0.1 broadcast_in_dim.31
  140.5 0.1 dynamic_update_slice.5
  140.6 9.4 %convolution_convert_fusion.3 = bf16[3072,3072]{1,0:T(8,128)(2,1)} fusion(bf16[6,32,3072]{2,1,0:T(8,128)(2,1)S(1)} %get-tuple-element.125, s32[]{:T(128)} %get-tuple-element.111, bf16[6,32,3072]{2,1,0:T(8,128)(2,1)S(1)} %get-tuple-element.122, bf16[6,32,32]{2,1,0:T(8,128)(2,1)S(1)} %get-tuple-element.124), kind=kOutput, calls=%fused_computation.3.clone.1 | convolution fusion | flops 619806720 | bytes 19277312 | tf_op jit(solution)/shard_map/while/body/eval_jaxpr/dot_general | solution.py:31
  150.0 14.8 %fusion.41 = f32[32,32]{1,0:T(8,128)S(1)} fusion(bf16[3072,3072]{1,0:T(8,128)(2,1)} %convolution_convert_fusion.3, bf16[3072,3072]{1,0:T(8,128)(2,1)} %get-tuple-element.123, bf16[6,32,3072]{2,1,0:T(8,128)(2,1)S(1)} %get-tuple-element.125, s32[]{:T(128)} %get-tuple-element.111, bf16[6,32,3072]{2,1,0:T(8,128)(2,1)S(1)} %get-tuple-element.122, ...), kind=kOutput, calls=%fused_computation.8.clone.1 | convolution fusion | flops 648120320 | bytes 38148096 | tf_op jit(solution)/shard_map/while/body/eval_jaxpr/dot_general | solution.py:41
  164.7 0.1 broadcast_in_dim.31
  164.8 0.1 dynamic_update_slice.5
  164.9 9.4 %convolution_convert_fusion.3 = bf16[3072,3072]{1,0:T(8,128)(2,1)} fusion(bf16[6,32,3072]{2,1,0:T(8,128)(2,1)S(1)} %get-tuple-element.125, s32[]{:T(128)} %get-tuple-element.111, bf16[6,32,3072]{2,1,0:T(8,128)(2,1)S(1)} %get-tuple-element.122, bf16[6,32,32]{2,1,0:T(8,128)(2,1)S(1)} %get-tuple-element.124), kind=kOutput, calls=%fused_computation.3.clone.1 | convolution fusion | flops 619806720 | bytes 19277312 | tf_op jit(solution)/shard_map/while/body/eval_jaxpr/dot_general | solution.py:31
  174.3 14.8 %fusion.41 = f32[32,32]{1,0:T(8,128)S(1)} fusion(bf16[3072,3072]{1,0:T(8,128)(2,1)} %convolution_convert_fusion.3, bf16[3072,3072]{1,0:T(8,128)(2,1)} %get-tuple-element.123, bf16[6,32,3072]{2,1,0:T(8,128)(2,1)S(1)} %get-tuple-element.125, s32[]{:T(128)} %get-tuple-element.111, bf16[6,32,3072]{2,1,0:T(8,128)(2,1)S(1)} %get-tuple-element.122, ...), kind=kOutput, calls=%fused_computation.8.clone.1 | convolution fusion | flops 648120320 | bytes 38148096 | tf_op jit(solution)/shard_map/while/body/eval_jaxpr/dot_general | solution.py:41
  189.0 0.1 broadcast_in_dim.31
  189.1 0.1 dynamic_update_slice.5
  189.2 9.4 %convolution_convert_fusion.3 = bf16[3072,3072]{1,0:T(8,128)(2,1)} fusion(bf16[6,32,3072]{2,1,0:T(8,128)(2,1)S(1)} %get-tuple-element.125, s32[]{:T(128)} %get-tuple-element.111, bf16[6,32,3072]{2,1,0:T(8,128)(2,1)S(1)} %get-tuple-element.122, bf16[6,32,32]{2,1,0:T(8,128)(2,1)S(1)} %get-tuple-element.124), kind=kOutput, calls=%fused_computation.3.clone.1 | convolution fusion | flops 619806720 | bytes 19277312 | tf_op jit(solution)/shard_map/while/body/eval_jaxpr/dot_general | solution.py:31
  198.6 14.8 %fusion.41 = f32[32,32]{1,0:T(8,128)S(1)} fusion(bf16[3072,3072]{1,0:T(8,128)(2,1)} %convolution_convert_fusion.3, bf16[3072,3072]{1,0:T(8,128)(2,1)} %get-tuple-element.123, bf16[6,32,3072]{2,1,0:T(8,128)(2,1)S(1)} %get-tuple-element.125, s32[]{:T(128)} %get-tuple-element.111, bf16[6,32,3072]{2,1,0:T(8,128)(2,1)S(1)} %get-tuple-element.122, ...), kind=kOutput, calls=%fused_computation.8.clone.1 | convolution fusion | flops 648120320 | bytes 38148096 | tf_op jit(solution)/shard_map/while/body/eval_jaxpr/dot_general | solution.py:41
  213.3 0.1 broadcast_in_dim.31
  213.4 0.1 dynamic_update_slice.5
  213.5 10.5 %psum.14 = f32[6,1024]{1,0:T(8,128)S(1)} all-reduce(f32[6,1024]{1,0:T(8,128)S(1)} %get-tuple-element.42), channel_id=1, replica_groups=mesh['pair'=2,'grow'=4,'gcol'=4] {'grow'}, use_global_device_ids=true, to_apply=%region_2.3 | all-reduce | flops 6144 | bytes 49152 | tf_op jit(solution)/shard_map/psum | solution.py:8
  224.0 17.3 %psum.15 = f32[6,1024]{1,0:T(8,128)S(1)} all-reduce(f32[6,1024]{1,0:T(8,128)S(1)} %psum.14), channel_id=1, replica_groups=mesh['pair'=2,'grow'=4,'gcol'=4] {'gcol'}, use_global_device_ids=true, to_apply=%region_3.4 | all-reduce | flops 6144 | bytes 49152 | tf_op jit(solution)/shard_map/psum | solution.py:8
  241.3 0.1 dynamic-slice_bitcast_fusion
  241.4 4.3 %all-gather = f32[2,6,64]{2,1,0:T(8,128)S(1)} all-gather(f32[1,6,64]{2,1,0:T(8,128)S(1)} %dynamic-slice_bitcast_fusion), channel_id=1, replica_groups=mesh['pair'=2,'grow'=4,'gcol'=4] {'pair'}, dimensions={0}, use_global_device_ids=true | all-gather | bytes 4608 | tf_op jit(solution)/shard_map/all_gather | solution.py:49
  245.8 0.6 gather_fusion
  246.3 0.7 broadcast_select_fusion
  (9 shorter events, 0.0 us)
Async XLA Ops:
  6.5 59.2 %all-gather.3.cloned.1.call-start = ((), (), s32[]{:S(2)}) async-start(), calls=%async_computation | async-start | bytes 5013504 | tf_op jit(solution)/shard_map/all_gather | solution.py:22
Sparse Core Ops, SparseCore 0:
  9.5 56.1 all-gather.2
